TPU v7x, 512 devices: a whole 4x4x16 slice. The times are simulated.
512 devices in a mesh: morton: 32 (over z_lo, x, core), lane: 16 (over z_hi, y).
Axes of the slice: x: 4, y: 4, z: 16 (z_hi: 4, z_lo: 4; z = z_hi * 4 + z_lo), core: 2. Of those that a mesh axis runs over, the one named last changes fastest.
Arguments:
- multipoles: bfloat16 [32, 2048, 296], P('morton', 'lane'), may hold values from -6 to 6
- counts: int32 [32, 2048], P('morton', 'lane'), may hold values from 1 to 48
- sources: int32 [32, 2048, 48], P('morton', 'lane'), may hold values from 0 to 1151, as said below
- relpos: int32 [32, 2048, 48], P('morton', 'lane'), may hold values from 0 to 47, as said below
- operators: bfloat16 [48, 296, 296], P('lane'), may hold values from -0.375 to 0.375
- c2e: bfloat16 [296, 296], replicated, may hold values from -0.375 to 0.375
Outputs:
- local_density: float32 [32, 2048, 296], P('morton', 'lane')
Inputs may be any that keep to these rules, and one draw needn't show every extreme that they name: `sources`: every live slot names a source box inside the grid of 32 x 16 devices' boxes. `relpos`: the ids of one box's slots are all different.
All inputs are finite; a program needn't handle non-finite values.
Results may differ from a plain program's by a relative error of at most 0.0029.
Values may be sent and summed in bfloat16 or wider, within the bound.
A program may use at most 64 MiB of HBM per device.

v0:
```python
import jax
import jax.numpy as jnp
from jax import lax
from jax.sharding import Mesh
from jax.sharding import PartitionSpec as P

LANE = ("lane_0", "lane_1")


group_width = 4


def with_halo(cells, sides, width):
    for axis, dim in sides:
        count = lax.axis_size(axis)
        ends = count - 1
        head = lax.slice_in_dim(cells, 0, width, axis=dim)
        tail = lax.slice_in_dim(cells, cells.shape[dim] - width, cells.shape[dim], axis=dim)
        cells = jnp.concatenate(
            [
                lax.ppermute(tail, axis, [(i, (i + 1) % count) for i in range(ends)]),
                cells,
                lax.ppermute(head, axis, [((i + 1) % count, i) for i in range(ends)]),
            ],
            axis=dim,
        )
    return cells


def joined_along(blocks, dim):
    blocks = jnp.moveaxis(blocks, 0, dim)
    lengths = blocks.shape
    return blocks.reshape(*lengths[:dim], lengths[dim] * lengths[dim + 1], *lengths[dim + 2 :])


def stacked_from(shard, axes, turns):
    blocks = shard
    for k in turns:
        blocks = lax.all_gather(blocks, axes[k])
    done = turns[::-1]
    back = [done.index(k) for k in range(len(axes))]
    blocks = blocks.transpose(*back, *range(len(axes), blocks.ndim))
    return blocks.reshape(-1, *shard.shape)


def gather_axes(shard, axes, turns, dim):
    return joined_along(stacked_from(shard, axes, turns), dim)


def per_device(multipoles, counts, sources, relpos, operators, c2e):
    box_count = multipoles.shape[1]
    width = multipoles.shape[2]
    block = multipoles.reshape(1, 1, box_count, width)
    padded = with_halo(block, (("morton", 0), (LANE, 1)), 1)
    table = padded.reshape(9 * box_count, width)
    codes = sources[0]
    rel_row = relpos[0]
    count_row = counts[0]
    slot_ids = lax.broadcasted_iota(jnp.int32, rel_row.shape, 1)
    live = slot_ids < count_row[:, None]

    def translate(total, matrices, hit):
        has = jnp.any(hit, axis=1)
        picked = jnp.sum(jnp.where(hit, codes[:, :, None], 0), axis=1)
        rows = table[picked.reshape(-1)].reshape(box_count, group_width, width)
        rows = jnp.where(has[:, :, None], rows, jnp.zeros((), table.dtype))
        return total + jnp.einsum("bgi,gij->bj", rows, matrices, preferred_element_type=jnp.float32)

    empty = jnp.zeros((box_count, width), jnp.float32)
    piece = gather_axes(operators, LANE, (0, 1), 0)
    length = piece.shape[0]
    groups = -(-length // group_width)
    padded_ops = piece
    padded_ops = padded_ops.reshape(groups, group_width, width, width)
    within = lax.broadcasted_iota(jnp.int32, (group_width,), 0)

    def turn(index, carry):
        matrices = lax.dynamic_index_in_dim(padded_ops, index, 0, keepdims=False)
        positions = index * group_width + within
        hit = live[:, :, None] & (rel_row[:, :, None] == positions[None, None, :])
        return translate(carry, matrices, hit)

    summed = lax.fori_loop(0, groups, turn, empty)
    check = summed.astype(jnp.bfloat16)
    density = jnp.dot(check, c2e, preferred_element_type=jnp.float32)
    return density.reshape(1, box_count, width)


def solution(mesh):
    finer = Mesh(mesh.devices.reshape(mesh.shape["morton"], 4, 4), ("morton", "lane_0", "lane_1"))
    in_specs = (
        P("morton", LANE, None),
        P("morton", LANE),
        P("morton", LANE, None),
        P("morton", LANE, None),
        P(LANE, None, None),
        P(),
    )
    out_specs = P("morton", LANE, None)
    return jax.shard_map(
        per_device, mesh=finer, in_specs=in_specs, out_specs=out_specs, check_vma=False
    )
```

profile of v0, /device:TPU:7, one launch (start us, length us, event | category | flops | bytes accessed | tf_op | source)
XLA Modules:
  0.0 318.9 jit_solution(13580978901246293919)
XLA Ops:
  7.3 124.2 %all-gather.5.cloned.1.call-done = bf16[12,296,296]{2,1,0:T(8,128)(2,1)} async-done(((bf16[3,296,296]{2,1,0:T(8,128)(2,1)}), bf16[12,296,296]{2,1,0:T(8,128)(2,1)}) %all-gather.5.cloned.1.call-update) | async-done | bytes 2102800 | tf_op jit(solution)/shard_map/all_gather | solution.py:39
  131.5 2.5 collective-permute-start.1
  134.0 5.2 %collective-permute-start = (bf16[1,1,128,296]{2,3,1,0:T(8,128)(2,1)}, bf16[1,1,128,296]{2,3,1,0:T(8,128)(2,1)S(1)}, u32[]{:S(2)}, u32[]{:S(2)}) collective-permute-start(bf16[1,1,128,296]{2,3,1,0:T(8,128)(2,1)} %bitcast.44), channel_id=1, source_target_pairs={{0,16},{16,32},{32,48},{48,64},{64,80},{80,96},{96,112},{112,128},... | collective-permute-start | bytes 227336 | tf_op jit(solution)/shard_map/ppermute | solution.py:21
  143.2 4.0 %collective-permute-start.2 = (bf16[3,1,128,296]{2,3,1,0:T(8,128)(2,1)S(1)}, bf16[3,1,128,296]{2,3,1,0:T(8,128)(2,1)S(1)}, u32[]{:S(2)}, u32[]{:S(2)}) collective-permute-start(bf16[3,1,128,296]{2,3,1,0:T(8,128)(2,1)S(1)} %pad_maximum_fusion.1), channel_id=1, source_target_pairs={{0,1},{1,2},{2,3},{3,4},{4,5},{5,6},{6,7},{7,8},{8,9},{9,10},{10,1... | collective-permute-start | bytes 681992 | tf_op jit(solution)/shard_map/ppermute | solution.py:21
  147.2 2.8 collective-permute-done.3
  152.2 92.6 %all-gather.7.cloned.1.call-done = bf16[16,3,296,296]{3,2,1,0:T(8,128)(2,1)} async-done(((bf16[4,3,296,296]{3,2,1,0:T(8,128)(2,1)}), bf16[16,3,296,296]{3,2,1,0:T(8,128)(2,1)}) %all-gather.7.cloned.1.call-update) | async-done | bytes 8411152 | tf_op jit(solution)/shard_map/all_gather | solution.py:39
  244.8 9.7 %copy.31 = bf16[4,4,3,296,296]{4,3,2,1,0:T(8,128)(2,1)} copy(bf16[4,4,3,296,296]{4,3,2,0,1:T(8,128)(2,1)} %bitcast.38) | data formatting | bytes 16822272 | tf_op jit(solution)/shard_map/transpose | solution.py:42
  254.6 56.5 %while.14 = (s32[]{:T(128)}, f32[128,296]{0,1:T(8,128)S(1)}, s32[1,128,48]{1,2,0:T(8,128)S(1)}, s32[1,128,48]{1,2,0:T(8,128)S(1)}, bf16[1152,296]{1,0:T(8,128)(2...) while((s32[]{:T(128)}, f32[128,296]{0,1:T(8,128)S(1)}, ...), condition=%wide.region_3.4_spmd.clone, body=%wide.region_0.3_spmd.clone.sunk | while | flops 90125832 | bytes 3451579 | solution.py:83
  255.2 1.9 gather_fusion
  257.6 1.7 fusion.19
  259.9 1.9 gather_fusion
  264.7 1.9 gather_fusion
  269.4 1.9 gather_fusion
  274.1 1.9 gather_fusion
  278.8 1.9 gather_fusion
  281.2 1.7 fusion.19
  283.5 1.9 gather_fusion
  288.2 1.9 gather_fusion
  290.6 1.7 fusion.19
  292.9 1.9 gather_fusion
  297.6 1.9 gather_fusion
  302.4 1.9 gather_fusion
  304.7 1.7 fusion.19
  307.1 1.9 gather_fusion
  (161 shorter events, 33.4 us)
Async XLA Ops:
  6.5 304.6 %copy-start = (bf16[296,296]{1,0:T(8,128)(2,1)S(1)}, bf16[296,296]{1,0:T(8,128)(2,1)}, u32[]{:S(2)}) copy-start(bf16[296,296]{1,0:T(8,128)(2,1)} %param.13) | copy-start | bytes 525700
  6.5 125.0 %all-gather.5.cloned.1.call-start = ((), (), s32[]{:S(2)}) async-start(), calls=%async_computation | async-start | bytes 3409920 | tf_op jit(solution)/shard_map/all_gather | solution.py:39
  7.3 237.6 %all-gather.7.cloned.1.call-start = ((), (), s32[]{:S(2)}) async-start(), calls=%async_computation.1 | async-start | bytes 13639680 | tf_op jit(solution)/shard_map/all_gather | solution.py:39
  131.5 8.0 %collective-permute-start.1 = (bf16[1,1,128,296]{2,3,1,0:T(8,128)(2,1)}, bf16[1,1,128,296]{2,3,1,0:T(8,128)(2,1)S(1)}, u32[]{:S(2)}, u32[]{:S(2)}) collective-permute-start(bf16[1,1,128,296]{2,3,1,0:T(8,128)(2,1)} %bitcast.43), channel_id=1, source_target_pairs={{16,0},{32,16},{48,32},{64,48},{80,64},{96,80},{112,96},{128,112},... | collective-permute-start | bytes 227336 | tf_op jit(solution)/shard_map/ppermute | solution.py:23
  134.0 6.9 %collective-permute-start = (bf16[1,1,128,296]{2,3,1,0:T(8,128)(2,1)}, bf16[1,1,128,296]{2,3,1,0:T(8,128)(2,1)S(1)}, u32[]{:S(2)}, u32[]{:S(2)}) collective-permute-start(bf16[1,1,128,296]{2,3,1,0:T(8,128)(2,1)} %bitcast.44), channel_id=1, source_target_pairs={{0,16},{16,32},{32,48},{48,64},{64,80},{80,96},{96,112},{112,128},... | collective-permute-start | bytes 227336 | tf_op jit(solution)/shard_map/ppermute | solution.py:21
  141.9 8.1 %collective-permute-start.3 = (bf16[3,1,128,296]{2,3,1,0:T(8,128)(2,1)S(1)}, bf16[3,1,128,296]{2,3,1,0:T(8,128)(2,1)S(1)}, u32[]{:S(2)}, u32[]{:S(2)}) collective-permute-start(bf16[3,1,128,296]{2,3,1,0:T(8,128)(2,1)S(1)} %pad_maximum_fusion.1), channel_id=1, source_target_pairs={{1,0},{2,1},{3,2},{4,3},{5,4},{6,5},{7,6},{8,7},{9,8},{10,9},{11,1... | collective-permute-start | bytes 681992 | tf_op jit(solution)/shard_map/ppermute | solution.py:23
  143.2 7.7 %collective-permute-start.2 = (bf16[3,1,128,296]{2,3,1,0:T(8,128)(2,1)S(1)}, bf16[3,1,128,296]{2,3,1,0:T(8,128)(2,1)S(1)}, u32[]{:S(2)}, u32[]{:S(2)}) collective-permute-start(bf16[3,1,128,296]{2,3,1,0:T(8,128)(2,1)S(1)} %pad_maximum_fusion.1), channel_id=1, source_target_pairs={{0,1},{1,2},{2,3},{3,4},{4,5},{5,6},{6,7},{7,8},{8,9},{9,10},{10,1... | collective-permute-start | bytes 681992 | tf_op jit(solution)/shard_map/ppermute | solution.py:21
  244.8 9.7 %copy-start.1 = (s32[1,128,48]{1,2,0:T(8,128)S(1)}, s32[1,128,48]{1,2,0:T(8,128)}, u32[]{:S(2)}) copy-start(s32[1,128,48]{1,2,0:T(8,128)} %param.11) | copy-start | bytes 73732
  244.8 9.7 %copy-start.2 = (s32[1,128,48]{1,2,0:T(8,128)S(1)}, s32[1,128,48]{1,2,0:T(8,128)}, u32[]{:S(2)}) copy-start(s32[1,128,48]{1,2,0:T(8,128)} %param.10) | copy-start | bytes 73732
  244.8 9.7 %copy-start.3 = (s32[1,128]{1,0:T(1,128)S(1)}, s32[1,128]{1,0:T(1,128)}, u32[]{:S(2)}) copy-start(s32[1,128]{1,0:T(1,128)} %param.9) | copy-start | bytes 1540
Sparse Core Ops, SparseCore 0:
  9.4 122.0 all-gather.4
  133.6 111.1 all-gather.6
where the time goes:
time: 321 us; the launch traced here: 319 us
  waiting for transfers between devices  223 us (69%)
  local copies, waits for them, and re-layouts  39 us (12%)
  matrix products  21.3 us (7%)
  between operations  13.5 us (4%)
  starting transfers between devices  13 us (4%)
  other arithmetic  8.21 us (3%)
    all_gather x2, waiting for transfers between devices, stacked_from(): blocks = lax.all_gather(blocks, axes[k])  217 us
    gather x24, local copies, waits for them, and re-layouts, translate(): rows = table[picked.reshape(-1)].reshape(box_count, group_width, width)  24.6 us
    dot_general x12, matrix products, translate(): jnp.einsum('bgi,gij->bj', rows, matrices, preferred_element_type=jnp.floa...  20.3 us
    transpose x1, local copies, waits for them, and re-layouts, stacked_from(): blocks = blocks.transpose(*back, *range(len(axes), blocks.ndim))  9.73 us
    ppermute x2, starting transfers between devices, with_halo(): lax.ppermute(tail, axis, [(i, (i + 1) % count) for i in range(ends)])  9.17 us
  transfers between devices with their start and end apart: 6, of which 6 were waited for; matrix products, arithmetic and copies ran while one was open for 1% of the time, Pallas kernels for 0%

commit v1 on v0

v1 whole, which is shorter than its diff:
```python
import jax
import jax.numpy as jnp
from jax import lax
from jax.experimental import pallas as pl
from jax.experimental.pallas import tpu as pltpu
from jax.sharding import Mesh
from jax.sharding import PartitionSpec as P

MESH = pl.DeviceIdType.MESH
F32 = jnp.float32
BF16 = jnp.bfloat16
MORTON = ("zl", "x", "core")
LANE = ("zh", "y")

RP = 320
RM = 304
PW = 896


def block_at(slot, a):
    return pl.ds(pl.multiple_of(128 * (3 * slot + a), 128), 128)


def kernel(mult, cnt, src, rel, ops, c2e, out, wide, pko, pk, tb, op, rem, rows, acc, ps, pr, send, recv):
    zl, x, c = lax.axis_index("zl"), lax.axis_index("x"), lax.axis_index("core")
    h, y = lax.axis_index("zh"), lax.axis_index("y")
    step = 1 - 2 * c
    m = (zl * 4 + x) * 2 + c

    def at_morton(k):
        k = lax.rem(k + 32, 32)
        return {"zl": k // 8, "x": lax.rem(k // 2, 4), "core": lax.rem(k, 2)}

    def at_y(d):
        return {"y": lax.rem(y + d + 4, 4)}

    def at_x(d):
        return {"x": lax.rem(x + d + 4, 4)}

    def at_h(d):
        return {"zh": lax.rem(h + d + 4, 4)}

    up, down = at_morton(m + 1), at_morton(m - 1)
    other = {"core": 1 - c}

    barrier = pltpu.get_barrier_semaphore()
    partners = [at_y(1), at_y(2), at_y(3), up, down, at_h(1), at_h(3), at_x(1), at_x(3)]
    partners += [{"zh": lax.rem(h + 3, 4), "y": 3}, {"zh": lax.rem(h + 1, 4), "y": 0}]
    for who in partners:
        pl.semaphore_signal(barrier, inc=1, device_id=who, device_id_type=MESH)

    def copy(n, src_ref, dst_ref, who, s=None):
        return pltpu.make_async_remote_copy(
            src_ref=src_ref, dst_ref=dst_ref, send_sem=send.at[n if s is None else s], recv_sem=recv.at[n],
            device_id=who, device_id_type=MESH,
        )

    wide[...] = jnp.zeros_like(wide)
    own = block_at(1 + y, 1)
    wide[0:128, 0:296] = mult[0].astype(F32)
    tb[:, own] = wide[0:128, :].T[0:RP].astype(BF16)
    for e in range(3):
        wide[0:296, 0:296] = ops[e].astype(F32)
        turned = wide[...].T
        op[0, :, 256 * e : 256 * e + 256] = turned[0:RP, 0:256].astype(BF16)
        last = turned[0:RP, 256:384]
        if e == 0:
            rest = last
        else:
            rest = rest + pltpu.roll(last, 40 * e, 1)
    op[0, :, 768:896] = rest.astype(BF16)
    wide[...] = jnp.zeros_like(wide)
    wide[0:128, 0:48] = rel[0].astype(F32)
    code = src[0]
    near = code >> 7
    a_of = (near * 11) >> 5
    b_of = near - 3 * a_of
    wide[0:128, 128:176] = ((b_of * 3 + a_of) * 128 + (code & 127)).astype(F32)
    relt = wide[0:128, 0:128].T[0:48]
    codet = wide[0:128, 128:256].T[0:48]
    live = lax.broadcasted_iota(jnp.int32, (48, 128), 0) < cnt[...]
    code1 = jnp.where(live, codet + 1.0, 0.0)
    pko[...] = jnp.zeros_like(pko)
    for yp in range(4):
        for s, off in enumerate((0, 3, 1, 2)):
            base = 12 * lax.rem(h + off, 4) + 3 * yp
            for e in range(3):
                want = (base + e).astype(F32)
                pko[yp, 3 * s + e : 3 * s + e + 1, :] = (
                    jnp.sum(jnp.where(relt == want, code1, 0.0), axis=0, keepdims=True) - 1.0
                )
    rem[...] = jnp.zeros_like(rem)

    is_end = ((y == 0) | (y == 3)).astype(jnp.int32)
    pl.semaphore_wait(barrier, 9 + 4 * is_end)

    xs = pl.ds(pl.multiple_of(80 * x, 16), 80)

    def xrows(d):
        return pl.ds(pl.multiple_of(80 * lax.rem(x + d + 4, 4), 16), 80)

    def erows(d):
        return pl.ds(pl.multiple_of(80 * lax.rem(y + d + 4, 4), 16), 80)

    started = []

    def go(cp):
        cp.start()
        started.append(cp)

    h_first = copy(0, op.at[0, xs], op.at[1 + c, xs], at_h(step))
    go(h_first)

    end0, end5 = block_at(0, 1), block_at(5, 1)

    @pl.when(y == 3)
    def _():
        for q in range(4):
            r = pl.ds(80 * q, 80)
            copy(1, tb.at[r, own], tb.at[r, end0], {"zh": lax.rem(h + 1, 4), "y": q}, s=60 + q).start()

    @pl.when(y == 0)
    def _():
        for q in range(4):
            r = pl.ds(80 * q, 80)
            copy(2, tb.at[r, own], tb.at[r, end5], {"zh": lax.rem(h + 3, 4), "y": q}, s=60 + q).start()

    def yblock(n, d, to):
        col = block_at(1 + lax.rem(y + d + 4, 4), 1)
        return copy(n, tb.at[:, col], tb.at[:, col], at_y(to))

    go(yblock(3, 0, 1))
    go(yblock(4, 0, -1))
    for d in (1, 2, 3):
        who = at_y(d)
        go(copy(4 + d, pko.at[who["y"]], pk.at[y], who))

    def mblock(n, slot, up_or_down):
        if up_or_down > 0:
            return copy(n, tb.at[:, block_at(slot, 1)], tb.at[:, block_at(slot, 0)], up)
        return copy(n, tb.at[:, block_at(slot, 1)], tb.at[:, block_at(slot, 2)], down)

    def mpair(n, slot):
        go(mblock(n, slot, 1))
        go(mblock(n + 1, slot, -1))

    def mwait(n, slot):
        copy(n, tb.at[:, block_at(slot, 0)], tb.at[:, block_at(slot, 0)], up).wait_recv()
        copy(n + 1, tb.at[:, block_at(slot, 2)], tb.at[:, block_at(slot, 2)], up).wait_recv()

    mpair(10, 1 + y)
    ybehind = lax.rem(y - step + 4, 4)
    yahead = lax.rem(y + step + 4, 4)
    yfar = lax.rem(y + 2, 4)

    def ywait(n, yy):
        col = block_at(1 + yy, 1)
        copy(n, tb.at[:, col], tb.at[:, col], at_y(1)).wait_recv()

    def ywait_two():
        ywait(3, lax.rem(y + 3, 4))
        ywait(4, lax.rem(y + 1, 4))

    ywait_two()
    colb = block_at(1 + ybehind, 1)
    go(copy(8, tb.at[:, colb], tb.at[:, colb], at_y(step)))
    mpair(12, 1 + ybehind)
    mpair(14, 1 + yahead)
    ywait(8, yfar)
    mpair(16, 1 + yfar)

    eh = erows(0)
    copy(1, tb.at[eh, end0], tb.at[eh, end0], at_y(1)).wait_recv()
    copy(2, tb.at[eh, end5], tb.at[eh, end5], at_y(1)).wait_recv()
    for d in (1, 2, 3):
        go(copy(17 + d, tb.at[eh, end0], tb.at[eh, end0], at_y(d)))
        go(copy(20 + d, tb.at[eh, end5], tb.at[eh, end5], at_y(d)))
    for d in (1, 2, 3):
        e = erows(-d)
        copy(17 + d, tb.at[e, end0], tb.at[e, end0], at_y(d)).wait_recv()
        copy(20 + d, tb.at[e, end5], tb.at[e, end5], at_y(d)).wait_recv()
    mpair(24, 0)
    mpair(26, 5)

    def opslice(slot, r, lanes):
        return op.at[slot, r, lanes] if lanes is not None else op.at[slot, r]

    def op_wait(n, slot, r, lanes):
        ref = opslice(slot, r, lanes)
        copy(n, ref, ref, other).wait_recv()

    def op_send(n, slot, r, lanes, who):
        ref = opslice(slot, r, lanes)
        return copy(n, ref, ref, who)

    mine = 1 + c
    op_wait(0, mine, xs, None)
    LO, HI = pl.ds(0, 512), pl.ds(512, 384)

    @pl.when(c == 0)
    def _():
        copy(30, op.at[1, xs, LO], op.at[3, xs, LO], at_h(1)).start()

    @pl.when(c == 1)
    def _():
        copy(30, op.at[2, xs, HI], op.at[3, xs, HI], at_h(3)).start()

    def xstage(n, slot, lanes):
        op_send(n, slot, xs, lanes, at_x(1)).start()
        op_send(n + 1, slot, xs, lanes, at_x(-1)).start()
        op_send(n + 3, slot, xs, lanes, other).start()
        op_wait(n, slot, xrows(-1), lanes)
        op_wait(n + 1, slot, xrows(1), lanes)
        op_send(n + 2, slot, xrows(-step), lanes, at_x(step)).start()
        op_send(n + 4, slot, xrows(-1), lanes, other).start()
        op_send(n + 5, slot, xrows(1), lanes, other).start()
        op_wait(n + 2, slot, xrows(2), lanes)
        op_send(n + 6, slot, xrows(2), lanes, other).start()

    def xsent(n, slot, lanes):
        for k, d in ((0, 0), (1, 0), (2, 0), (3, 0), (4, -1), (5, 1), (6, 2)):
            op_send(n + k, slot, xrows(d), lanes, other).wait_send()

    def cwait(n, slot, lanes):
        for k, d in ((3, 0), (4, -1), (5, 1), (6, 2)):
            op_wait(n + k, slot, xrows(d), lanes)

    xstage(31, mine, None)

    @pl.when(c == 0)
    def _():
        op_wait(30, 3, xs, LO)
        xstage(38, 3, LO)
        xsent(38, 3, LO)
        op_send(30, 3, xs, LO, other).wait_send()

    @pl.when(c == 1)
    def _():
        op_wait(30, 3, xs, HI)
        xstage(38, 3, HI)
        xsent(38, 3, HI)
        op_send(30, 3, xs, HI, other).wait_send()

    pk[y] = pko[y]
    for d in (1, 2, 3):
        copy(4 + d, pko.at[0], pk.at[lax.rem(y - d + 4, 4)], at_y(d)).wait_recv()
    mwait(10, 1 + y)
    mwait(12, 1 + ybehind)
    mwait(14, 1 + yahead)
    mwait(16, 1 + yfar)
    mwait(24, 0)
    mwait(26, 5)

    place = lax.broadcasted_iota(jnp.int32, (1152, 128), 0).astype(F32)

    def gather(lam, _):
        cols = pl.ds(pl.multiple_of(384 * lam, 128), 1152)
        to = pl.ds(pl.multiple_of(128 * lam, 128), 128)

        def pair(s, _):
            for e in range(3):
                want = pk[lam, pl.ds(3 * s + e, 1), :]
                hot = jnp.where(place == want, 1.0, 0.0).astype(BF16)
                got = jnp.dot(tb[0:RM, cols], hot, preferred_element_type=F32)
                rows[s, 256 * e : 256 * e + 256, to] = got[0:256].astype(BF16)
                rem[s, 40 * e : 40 * e + 40, to] = got[256:296]
            return 0

        lax.fori_loop(0, 4, pair, 0)
        return 0

    lax.fori_loop(0, 4, gather, 0)

    @pl.when(c == 0)
    def _():
        cwait(31, 2, None)
        cwait(38, 3, HI)

    @pl.when(c == 1)
    def _():
        cwait(31, 1, None)
        cwait(38, 3, LO)

    xsent(31, mine, None)
    for s in range(4):
        rows[s, 768:896, :] = rem[s].astype(BF16)
        part = jnp.dot(op[s, 0:RM, :], rows[s], preferred_element_type=F32)
        if s == 0:
            acc[...] = part
        else:
            acc[...] += part

    for lam in range(4):
        ps[lam] = acc[:, 128 * lam : 128 * lam + 128].astype(BF16)
    for d in (1, 2, 3):
        who = at_y(d)
        go(copy(45 + d, ps.at[who["y"]], pr.at[d - 1], who))
    total = acc[:, pl.ds(pl.multiple_of(128 * y, 128), 128)]
    for d in (1, 2, 3):
        copy(45 + d, ps.at[0], pr.at[d - 1], at_y(d)).wait_recv()
    for d in range(3):
        total = total + pr[d].astype(F32)
    wide[0:RM, 0:128] = total
    wide[RM:384, 0:128] = jnp.zeros((384 - RM, 128), F32)
    check = wide[:, 0:128].T
    high = check.astype(BF16)
    low = (check - high.astype(F32)).astype(BF16)
    out[0] = jnp.dot(high[:, 0:296], c2e[...], preferred_element_type=F32) + jnp.dot(
        low[:, 0:296], c2e[...], preferred_element_type=F32
    )

    for cp in started:
        cp.wait_send()

    @pl.when(y == 3)
    def _():
        for q in range(4):
            r = pl.ds(80 * q, 80)
            copy(1, tb.at[r, own], tb.at[r, end0], at_h(1), s=60 + q).wait_send()

    @pl.when(y == 0)
    def _():
        for q in range(4):
            r = pl.ds(80 * q, 80)
            copy(2, tb.at[r, own], tb.at[r, end5], at_h(1), s=60 + q).wait_send()


def per_device(multipoles, counts, sources, relpos, operators, c2e):
    vmem = pl.BlockSpec(memory_space=pltpu.VMEM)
    return pl.pallas_call(
        kernel,
        out_shape=jax.ShapeDtypeStruct((1, 128, 296), F32),
        in_specs=[vmem] * 6,
        out_specs=vmem,
        scratch_shapes=[
            pltpu.VMEM((384, 384), F32),
            pltpu.VMEM((4, 16, 128), F32),
            pltpu.VMEM((4, 16, 128), F32),
            pltpu.VMEM((RP, 18 * 128), BF16),
            pltpu.VMEM((4, RP, PW), BF16),
            pltpu.VMEM((4, 128, 512), F32),
            pltpu.VMEM((4, PW, 512), BF16),
            pltpu.VMEM((RM, 512), F32),
            pltpu.VMEM((4, RM, 128), BF16),
            pltpu.VMEM((3, RM, 128), BF16),
            pltpu.SemaphoreType.DMA((64,)),
            pltpu.SemaphoreType.DMA((64,)),
        ],
        compiler_params=pltpu.CompilerParams(collective_id=0, has_side_effects=True, vmem_limit_bytes=48 * 1024 * 1024),
    )(multipoles, counts, sources, relpos, operators, c2e)


def solution(mesh):
    finer = Mesh(mesh.devices.reshape(4, 4, 2, 4, 4), MORTON + LANE)
    in_specs = (
        P(MORTON, LANE, None),
        P(MORTON, LANE),
        P(MORTON, LANE, None),
        P(MORTON, LANE, None),
        P(LANE, None, None),
        P(),
    )
    return jax.shard_map(
        per_device, mesh=finer, in_specs=in_specs, out_specs=P(MORTON, LANE, None), check_vma=False
    )
```

time: 321 us -> 81.7 us (0.25)
  the two profiles are of different devices: /device:TPU:7 before, /device:TPU:2 now
where the time goes in v1:
time: 81.7 us; the launch traced here: 81.4 us
  Pallas kernels  76.8 us (94%)
  local copies, waits for them, and re-layouts  4.59 us (6%)
    pallas_call x1, Pallas kernels, per_device(): pl.pallas_call(kernel, out_shape=jax.ShapeDtypeStruct((1, 128, 296), F32)...  76.8 us
    unnamed x9, local copies, waits for them, and re-layouts  3.81 us

profile of v1, /device:TPU:2, one launch (start us, length us, event | category | flops | bytes accessed | tf_op | source)
XLA Modules:
  0.0 81.4 jit_solution(4677848355334809702)
XLA Ops:
  0.0 0.0 copy-start.1
  0.0 0.9 %copy.8.src = s32[1,128,48]{2,1,0:T(8,128)S(1)} copy(s32[1,128,48]{1,2,0:T(8,128)} %param.8) | data formatting | bytes 49152 | tf_op args[2]
  0.9 0.8 %copy.9.rel = s32[1,128,48]{2,1,0:T(8,128)S(1)} copy(s32[1,128,48]{1,2,0:T(8,128)} %param.9) | data formatting | bytes 49152 | tf_op args[3]
  1.7 0.0 copy-start.2
  1.7 1.0 %copy.7.mult = bf16[1,128,296]{2,1,0:T(8,128)(2,1)S(1)} copy(bf16[1,128,296]{1,2,0:T(8,128)(2,1)} %param.6) | data formatting | bytes 151552 | tf_op args[0]
  2.7 0.0 copy-done.1
  2.7 0.0 copy-done.2
  2.8 0.0 copy-start
  2.8 1.1 %copy-done = bf16[3,296,296]{2,1,0:T(8,128)(2,1)S(1)} copy-done((bf16[3,296,296]{2,1,0:T(8,128)(2,1)S(1)}, bf16[3,296,296]{2,1,0:T(8,128)(2,1)}, u32[]{:S(2)}) %copy-start) | copy-done | bytes 525720
  3.9 76.8 %shard_map.64 = f32[1,128,296]{2,1,0:T(8,128)S(1)} custom-call(bf16[1,128,296]{2,1,0:T(8,128)(2,1)S(1)} %copy.7.mult, s32[1,128]{1,0:T(1,128)S(1)} %copy-done.2, s32[1,128,48]{2,1,0:T(8,128)S(1)} %copy.8.src, s32[1,128,48]{2,1,0:T(8,128)S(1)} %copy.9.rel, bf16[3,296,296]{2,1,0:T(8,128)(2,1)S(1)} %copy-done, bf16[296,296]{1,0:T(8,128)(2,1)S(1)} %copy-done.1), custom_call_target="tpu_custom_call" | custom-call | tf_op jit(solution)/shard_map/pallas_call | solution.py:330
  80.7 0.8 copy.10
Async XLA Ops:
  0.0 2.7 %copy-start.1 = (bf16[296,296]{1,0:T(8,128)(2,1)S(1)}, bf16[296,296]{1,0:T(8,128)(2,1)}, u32[]{:S(2)}) copy-start(bf16[296,296]{1,0:T(8,128)(2,1)} %c2e.1) | copy-start | bytes 525700
  1.7 1.0 %copy-start.2 = (s32[1,128]{1,0:T(1,128)S(1)}, s32[1,128]{1,0:T(1,128)}, u32[]{:S(2)}) copy-start(s32[1,128]{1,0:T(1,128)} %cnt.1) | copy-start | bytes 1540
  2.8 1.1 %copy-start = (bf16[3,296,296]{2,1,0:T(8,128)(2,1)S(1)}, bf16[3,296,296]{2,1,0:T(8,128)(2,1)}, u32[]{:S(2)}) copy-start(bf16[3,296,296]{2,1,0:T(8,128)(2,1)} %ops.1) | copy-start | bytes 1577092
